TPU v7x, 32 devices: a whole 2x2x4 slice. The times are simulated.
32 devices in a mesh: gy: 8 (over z, x), gz: 4 (over y, core).
Axes of the slice: x: 2, y: 2, z: 4, core: 2. Of those that a mesh axis runs over, the one named last changes fastest.
Arguments:
- tokens: bfloat16 [16, 64, 16, 192], P(None, 'gy', 'gz'), may hold values from -36 to 36
- qkv_weight: bfloat16 [192, 576], replicated, may hold values from -0.4375 to 0.4375
- out_weight: bfloat16 [192, 192], replicated, may hold values from -1.25 to 1.25
- conv_kernel: float32 [3, 3, 3, 192], replicated, may hold values from -1.25 to 1.25
- up_weight: bfloat16 [192, 768], replicated, may hold values from -0.4375 to 0.4375
- down_weight: bfloat16 [768, 192], replicated, may hold values from -0.21875 to 0.21875
- band_mask: int32 [4, 4], replicated, may hold values from 0 to 1, as said below
- grad_out: bfloat16 [16, 64, 16, 192], P(None, 'gy', 'gz'), may hold values from -6 to 6
Outputs:
- block_out: bfloat16 [16, 64, 16, 192], P(None, 'gy', 'gz')
- token_gradient: bfloat16 [16, 64, 16, 192], P(None, 'gy', 'gz')
- qkv_gradient: float32 [192, 576], replicated
- out_gradient: float32 [192, 192], replicated
- kernel_gradient: float32 [3, 3, 3, 192], replicated
- up_gradient: float32 [192, 768], replicated
- down_gradient: float32 [768, 192], replicated
Inputs may be any that keep to these rules, and one draw needn't show every extreme that they name: band_mask[i, i] is 1, and band_mask[i, j] is 0 where |i - j| > 4; other entries are 0 or 1.
All inputs are finite; a program needn't handle non-finite values.
Results may differ from a plain program's by a relative error of at most 0.017.
Values may be sent and summed in bfloat16 or wider, within the bound.
A program may use at most 64 MiB of HBM per device.

v0:
```python
import math
import jax
import jax.numpy as jnp
from jax import lax
from jax.sharding import PartitionSpec as P

HEADS = 6
BLOCK = 16
NORM_EPS = 1e-05
UNIT_EPS = 1e-06
GELU_SLOPE = 0.7978845608028654
GELU_CUBIC = 0.044715


def with_halo(cells, sides, width):
    for axis, dim in sides:
        count = lax.axis_size(axis)
        head = lax.slice_in_dim(cells, 0, width, axis=dim)
        tail = lax.slice_in_dim(cells, cells.shape[dim] - width, cells.shape[dim], axis=dim)
        cells = jnp.concatenate(
            [
                lax.ppermute(tail, axis, [(i, (i + 1) % count) for i in range(count)]),
                cells,
                lax.ppermute(head, axis, [((i + 1) % count, i) for i in range(count)]),
            ],
            axis=dim,
        )
    return cells


def norm_rows(values):
    centred = values - jnp.mean(values, axis=-1, keepdims=True)
    inverse = lax.rsqrt(jnp.mean(centred * centred, axis=-1, keepdims=True) + NORM_EPS)
    return (centred * inverse, inverse)


def norm_rows_back(upstream, normal, inverse):
    return inverse * (
        upstream
        - jnp.mean(upstream, axis=-1, keepdims=True)
        - normal * jnp.mean(upstream * normal, axis=-1, keepdims=True)
    )


def unit_scale(values):
    return lax.rsqrt(jnp.mean(values * values, axis=-1, keepdims=True) + UNIT_EPS)


def unit_back(upstream, values, scaling):
    return scaling * upstream - scaling * scaling * scaling * values * jnp.mean(
        upstream * values, axis=-1, keepdims=True
    )


def gelu_value(pre_act):
    return (
        0.5
        * pre_act
        * (1.0 + jnp.tanh(GELU_SLOPE * (pre_act + GELU_CUBIC * pre_act * pre_act * pre_act)))
    )


def gelu_slope(pre_act):
    tangent = jnp.tanh(GELU_SLOPE * (pre_act + GELU_CUBIC * pre_act * pre_act * pre_act))
    return 0.5 * (1.0 + tangent) + 0.5 * pre_act * (1.0 - tangent * tangent) * GELU_SLOPE * (
        1.0 + 3.0 * GELU_CUBIC * pre_act * pre_act
    )


def flatten_rows(values):
    return values.reshape(-1, values.shape[-1])


def project(values, weight):
    summed = jnp.dot(flatten_rows(values), weight, preferred_element_type=jnp.float32)
    return summed.reshape(values.shape[:-1] + (weight.shape[1],))


def project_back(values, weight):
    summed = lax.dot_general(
        flatten_rows(values), weight, (((1,), (1,)), ((), ())), preferred_element_type=jnp.float32
    )
    return summed.reshape(values.shape[:-1] + (weight.shape[0],))


def contract(left_rows, right_rows):
    return lax.dot_general(
        flatten_rows(left_rows),
        flatten_rows(right_rows),
        (((0,), (0,)), ((), ())),
        preferred_element_type=jnp.float32,
    )


def split_heads(values, head_count):
    return values.reshape(values.shape[:-1] + (head_count, values.shape[-1] // head_count))


def join_heads(values):
    return values.reshape(values.shape[:-2] + (values.shape[-2] * values.shape[-1],))


def head_product(einsum_form, left_side, right_side):
    return jnp.einsum(einsum_form, left_side, right_side, preferred_element_type=jnp.float32)


def attention_parts(qkv_rows, mask_full, head_count):
    feature_width = qkv_rows.shape[-1] // 3
    query_vec = qkv_rows[..., :feature_width].astype(jnp.float32)
    key_vec = qkv_rows[..., feature_width : 2 * feature_width].astype(jnp.float32)
    query_scale = unit_scale(query_vec)
    key_scale = unit_scale(key_vec)
    query_unit = (query_vec * query_scale).astype(jnp.bfloat16)
    key_unit = (key_vec * key_scale).astype(jnp.bfloat16)
    factor = 2.0 / math.sqrt(feature_width // head_count)
    scores = head_product(
        "aibhd,ajbhd->abhij", split_heads(query_unit, head_count), split_heads(key_unit, head_count)
    )
    weights = mask_full * jnp.exp(factor * scores)
    attn_probs = weights / jnp.sum(weights, axis=-1, keepdims=True)
    return (query_vec, key_vec, query_scale, key_scale, query_unit, key_unit, attn_probs, factor)


def attend(qkv_rows, mask_full, head_count):
    query_vec, key_vec, query_scale, key_scale, query_unit, key_unit, attn_probs, factor = (
        attention_parts(qkv_rows, mask_full, head_count)
    )
    feature_width = qkv_rows.shape[-1] // 3
    value_heads = split_heads(qkv_rows[..., 2 * feature_width :], head_count)
    probs_low = attn_probs.astype(jnp.bfloat16)
    mixed_heads = head_product("abhij,ajbhd->aibhd", probs_low, value_heads)
    return join_heads(mixed_heads).astype(jnp.bfloat16)


def attend_back(qkv_rows, mask_full, head_count, upstream):
    query_vec, key_vec, query_scale, key_scale, query_unit, key_unit, attn_probs, factor = (
        attention_parts(qkv_rows, mask_full, head_count)
    )
    feature_width = qkv_rows.shape[-1] // 3
    value_heads = split_heads(qkv_rows[..., 2 * feature_width :], head_count)
    grad_heads = split_heads(upstream, head_count)
    probs_low = attn_probs.astype(jnp.bfloat16)
    grad_probs = head_product("aibhd,ajbhd->abhij", grad_heads, value_heads)
    grad_values = head_product("abhij,aibhd->ajbhd", probs_low, grad_heads)
    grad_scores = attn_probs * (
        grad_probs - jnp.sum(grad_probs * attn_probs, axis=-1, keepdims=True)
    )
    grad_low = (factor * grad_scores).astype(jnp.bfloat16)
    grad_qunit = join_heads(
        head_product("abhij,ajbhd->aibhd", grad_low, split_heads(key_unit, head_count))
    )
    grad_kunit = join_heads(
        head_product("abhij,aibhd->ajbhd", grad_low, split_heads(query_unit, head_count))
    )
    grad_query = unit_back(grad_qunit, query_vec, query_scale).astype(jnp.bfloat16)
    grad_key = unit_back(grad_kunit, key_vec, key_scale).astype(jnp.bfloat16)
    return jnp.concatenate(
        [grad_query, grad_key, join_heads(grad_values).astype(jnp.bfloat16)], axis=-1
    )


def conv_apply(padded, kernel_taps):
    extent_x = padded.shape[0] - 2
    extent_y = padded.shape[1] - 2
    extent_z = padded.shape[2] - 2
    summed = jnp.zeros((extent_x, extent_y, extent_z, padded.shape[3]), jnp.float32)
    for shift_x in range(3):
        for shift_y in range(3):
            for shift_z in range(3):
                window = padded[
                    shift_x : shift_x + extent_x,
                    shift_y : shift_y + extent_y,
                    shift_z : shift_z + extent_z,
                ]
                summed = summed + kernel_taps[shift_x, shift_y, shift_z] * window.astype(
                    jnp.float32
                )
    return summed


def kernel_grad(padded, upstream):
    extent_x, extent_y, extent_z, channels = upstream.shape
    upstream_wide = upstream.astype(jnp.float32)
    pieces = []
    for shift_x in range(3):
        for shift_y in range(3):
            for shift_z in range(3):
                window = padded[
                    shift_x : shift_x + extent_x,
                    shift_y : shift_y + extent_y,
                    shift_z : shift_z + extent_z,
                ]
                pieces.append(jnp.sum(window.astype(jnp.float32) * upstream_wide, axis=(0, 1, 2)))
    return jnp.stack(pieces).reshape(3, 3, 3, channels)


def mlp_pass(mixed_field, upstream, up_weight, down_weight):
    mixed_wide = mixed_field.astype(jnp.float32)
    normal, inverse = norm_rows(mixed_wide)
    normed = normal.astype(jnp.bfloat16)
    pre_act = project(normed, up_weight)
    hidden = gelu_value(pre_act).astype(jnp.bfloat16)
    block_out = (mixed_wide + project(hidden, down_weight)).astype(jnp.bfloat16)
    grad_hidden = project_back(upstream, down_weight).astype(jnp.bfloat16)
    part_down = contract(hidden, upstream)
    grad_pre = (grad_hidden.astype(jnp.float32) * gelu_slope(pre_act)).astype(jnp.bfloat16)
    part_up = contract(normed, grad_pre)
    grad_normed = project_back(grad_pre, up_weight)
    grad_mixed = (
        upstream.astype(jnp.float32) + norm_rows_back(grad_normed, normal, inverse)
    ).astype(jnp.bfloat16)
    return (block_out, grad_mixed, part_up, part_down)


def attention_exchange_back(qkv_lines, mask_full):
    return lax.all_to_all(
        attend(qkv_lines, mask_full, HEADS), "gy", split_axis=1, concat_axis=0, tiled=True
    )


def extend_values(field_values):
    grown = with_halo(field_values, (("gy", 1), ("gz", 2)), 1)
    return jnp.pad(grown, ((1, 1), (0, 0), (0, 0), (0, 0)))


def extend_grads(field_values):
    grown = with_halo(field_values, (("gy", 1), ("gz", 2)), 1)
    return jnp.pad(grown, ((1, 1), (0, 0), (0, 0), (0, 0)))


def local(tokens, qkv_weight, out_weight, conv_kernel, up_weight, down_weight, band_mask, grad_out):
    block_count = band_mask.shape[0]
    line_length = block_count * BLOCK
    mask_full = (
        jnp.broadcast_to(band_mask[:, None, :, None], (block_count, BLOCK, block_count, BLOCK))
        .reshape(line_length, line_length)
        .astype(jnp.float32)
    )
    flipped = conv_kernel[::-1, ::-1, ::-1]
    token_wide = tokens.astype(jnp.float32)
    normal_first, inverse_first = norm_rows(token_wide)
    normed_first = normal_first.astype(jnp.bfloat16)
    qkv_rows = project(normed_first, qkv_weight).astype(jnp.bfloat16)
    line_items = lax.all_to_all(qkv_rows, "gy", split_axis=0, concat_axis=1, tiled=True)
    attended = attention_exchange_back(line_items, mask_full)
    value_field = (token_wide + project(attended, out_weight)).astype(jnp.bfloat16)
    padded_value = extend_values(value_field)
    mixed_field = (value_field.astype(jnp.float32) + conv_apply(padded_value, conv_kernel)).astype(
        jnp.bfloat16
    )
    block_out, grad_mixed, part_up, part_down = mlp_pass(
        mixed_field, grad_out, up_weight, down_weight
    )
    padded_grad = extend_grads(grad_mixed)
    grad_value = (grad_mixed.astype(jnp.float32) + conv_apply(padded_grad, flipped)).astype(
        jnp.bfloat16
    )
    part_kernel = kernel_grad(padded_value, grad_mixed)
    grad_attended = project_back(grad_value, out_weight).astype(jnp.bfloat16)
    part_out = contract(attended, grad_value)
    grad_lines = lax.all_to_all(grad_attended, "gy", split_axis=0, concat_axis=1, tiled=True)
    grad_qkv_lines = attend_back(line_items, mask_full, HEADS, grad_lines)
    grad_qkv_rows = lax.all_to_all(grad_qkv_lines, "gy", split_axis=1, concat_axis=0, tiled=True)
    grad_normed = project_back(grad_qkv_rows, qkv_weight).astype(jnp.bfloat16)
    part_qkv = contract(normed_first, grad_qkv_rows)
    token_gradient = (
        grad_value.astype(jnp.float32)
        + norm_rows_back(grad_normed.astype(jnp.float32), normal_first, inverse_first)
    ).astype(jnp.bfloat16)
    summed_parts = lax.psum((part_qkv, part_out, part_kernel, part_up, part_down), ("gy", "gz"))
    token_count = (
        tokens.shape[0]
        * tokens.shape[1]
        * lax.axis_size("gy")
        * tokens.shape[2]
        * lax.axis_size("gz")
    )
    factor = 1.0 / math.sqrt(token_count)
    return (
        block_out,
        token_gradient,
        summed_parts[0] * factor,
        summed_parts[1] * factor,
        summed_parts[2] * factor,
        summed_parts[3] * factor,
        summed_parts[4] * factor,
    )


def solution(mesh):
    placed = (P(None, "gy", "gz", None), P(), P(), P(), P(), P(), P(), P(None, "gy", "gz", None))
    return jax.shard_map(
        local,
        mesh=mesh,
        in_specs=placed,
        out_specs=(P(None, "gy", "gz", None), P(None, "gy", "gz", None), P(), P(), P(), P(), P()),
        check_vma=False,
    )
```

profile of v0, /device:TPU:0, one launch (start us, length us, event | category | flops | bytes accessed | tf_op | source)
XLA Modules:
  0.0 343.9 jit_solution(10555786560866475854)
XLA Ops:
  10.8 2.1 convolution_convert_fusion.1
  12.9 7.3 %all-to-all-start = ((bf16[16,8,4,576]{3,1,2,0:T(8,128)(2,1)}), bf16[16,8,4,576]{3,1,2,0:T(8,128)(2,1)S(1)}, u32[]{:S(2)}, u32[]{:S(2)}) async-start(bf16[16,8,4,576]{3,1,2,0:T(8,128)(2,1)} %convolution_convert_fusion.1), calls=%async_computation | async-start | bytes 1310720 | tf_op jit(solution)/shard_map/all_to_all | solution.py:244
  20.5 17.0 %all-to-all-done = bf16[16,8,4,576]{3,1,2,0:T(8,128)(2,1)S(1)} async-done(((bf16[16,8,4,576]{3,1,2,0:T(8,128)(2,1)}), bf16[16,8,4,576]{3,1,2,0:T(8,128)(2,1)S(1)}, u32[]{:S(2)}, u32[]{:S(2)}) %all-to-all-start) | async-done | bytes 589856 | tf_op jit(solution)/shard_map/all_to_all | solution.py:244
  41.0 1.6 exponential_multiply_fusion
  42.6 2.4 convolution_convert_fusion.3
  46.3 12.5 %all_to_all.63 = bf16[2,64,4,192]{3,2,0,1:T(4,128)(2,1)S(1)} all-to-all(bf16[2,64,4,192]{3,2,0,1:T(4,128)(2,1)S(1)} %copy.104), channel_id=1, replica_groups=mesh['gy'=8,'gz'=4] {'gy'}, dimensions={1} | all-to-all | bytes 393216 | tf_op jit(solution)/shard_map/all_to_all | solution.py:216
  59.3 1.5 collective-permute-start
  60.8 3.3 collective-permute-start.1
  64.8 1.5 collective-permute-done
  66.5 1.7 collective-permute-start.3
  72.8 2.4 convert_reduce_fusion
  78.3 1.8 fusion.121
  81.5 4.0 %collective-permute-start.5 = (bf16[16,1,4,192]{3,1,2,0:T(2,128)(2,1)}, bf16[16,1,4,192]{3,1,2,0:T(2,128)(2,1)S(1)}, u32[]{:S(2)}, u32[]{:S(2)}) collective-permute-start(bf16[16,1,4,192]{3,1,2,0:T(2,128)(2,1)} %get-tuple-element.96), channel_id=1, source_target_pairs={{4,0},{8,4},{12,8},{16,12},{20,16},{24,20},{28,24},{0,28},{5,1},{9... | collective-permute-start | bytes 73736 | tf_op jit(solution)/shard_map/ppermute | solution.py:24
  90.2 1.8 fusion.130
  95.2 2.2 fusion.132
  98.4 5.7 %all-to-all-start.2 = ((bf16[16,8,4,192]{3,1,2,0:T(8,128)(2,1)}), bf16[16,8,4,192]{3,1,2,0:T(8,128)(2,1)}, u32[]{:S(2)}, u32[]{:S(2)}) async-start(bf16[16,8,4,192]{3,1,2,0:T(8,128)(2,1)} %convolution_convert_fusion.4), calls=%async_computation.2 | async-start | bytes 524288 | tf_op jit(solution)/shard_map/all_to_all | solution.py:261
  104.2 2.2 fusion.18
  107.4 2.8 stack.111
  110.2 41.6 %psum.37 = f32[3,3,3,192]{3,2,1,0:T(4,128)S(1)} all-reduce(f32[3,3,3,192]{3,2,1,0:T(4,128)S(1)} %reshape.191), channel_id=1, replica_groups=mesh['gy'=8,'gz'=4] {'gy','gz'}, use_global_device_ids=true, to_apply=%region_43.44 | all-reduce | flops 5184 | bytes 41472 | tf_op jit(solution)/shard_map/psum | solution.py:270
  151.8 2.5 convolution_bitcast_fusion.1
  157.0 3.2 convolution_convert_fusion.2
  160.2 1.5 fusion.163
  161.8 3.3 fusion.16
  165.1 3.4 %fusion.13 = f32[2,4,6,32,64]{4,3,2,1,0:T(8,128)} fusion(bf16[2,64,4,6,32]{1,4,3,2,0:T(8,128)(2,1)} %bitcast.173, f32[2,4,6,64,64]{3,4,2,1,0:T(8,128)} %fusion.27, f32[2,4,6,64,64]{3,4,2,1,0:T(8,128)S(1)} %fusion.163), kind=kOutput, calls=%fused_computation.47 | convolution fusion | flops 13569087 | bytes 2162688 | tf_op jit(solution)/shard_map/abhij,aibhd->ajbhd/dot_general | solution.py:104
  169.7 1.4 copy.115
  171.2 1.4 copy.112
  173.9 1.3 copy.120
  175.2 5.2 %all-to-all-start.3 = ((bf16[2,64,4,576]{3,2,0,1:T(4,128)(2,1)}), bf16[2,64,4,576]{3,2,0,1:T(4,128)(2,1)S(1)}, u32[]{:S(2)}, u32[]{:S(2)}) async-start(bf16[2,64,4,576]{3,2,0,1:T(4,128)(2,1)} %copy.120), calls=%async_computation.3 | async-start | bytes 1310720 | tf_op jit(solution)/shard_map/all_to_all | solution.py:263
  183.7 12.4 %all-to-all-done.3 = bf16[2,64,4,576]{3,2,0,1:T(4,128)(2,1)S(1)} async-done(((bf16[2,64,4,576]{3,2,0,1:T(4,128)(2,1)}), bf16[2,64,4,576]{3,2,0,1:T(4,128)(2,1)S(1)}, u32[]{:S(2)}, u32[]{:S(2)}) %all-to-all-start.3) | async-done | bytes 589856 | tf_op jit(solution)/shard_map/all_to_all | solution.py:263
  200.5 131.3 %all-reduce.5.cloned.1.call-done = (f32[192,576]{1,0:T(8,128)}, f32[192,192]{1,0:T(8,128)}, f32[192,768]{1,0:T(8,128)}, f32[768,192]{0,1:T(8,128)}) async-done(((f32[192,576]{1,0:T(8,128)}, f32[192,192]{1,0:T(8,128)}, f32[192,768]{1,0:T(8,128)}, f32[768,192]{0,1:T(8,128)}), (f32[192,576]{1,0:T(8,128)}, f32[192,192]{1,0:T(8,128)}, f32[192,768]{1,0:T(8,128)}, ...) | async-done | bytes 1769488 | tf_op jit(solution)/shard_map/psum | solution.py:270
  331.8 1.9 broadcast_multiply_fusion.2
  333.7 1.6 broadcast_multiply_fusion.3
  (265 shorter events, 42.3 us)
Async XLA Ops:
  7.2 68.4 %copy-start = (bf16[192,768]{1,0:T(8,128)(2,1)S(1)}, bf16[192,768]{1,0:T(8,128)(2,1)}, u32[]{:S(2)}) copy-start(bf16[192,768]{1,0:T(8,128)(2,1)} %param.12) | copy-start | bytes 884740
  9.6 10.6 %copy-start.85 = (s32[4,4]{1,0:T(4,128)S(1)}, s32[4,4]{1,0:T(4,128)}, u32[]{:S(2)}) copy-start(s32[4,4]{1,0:T(4,128)} %param.14) | copy-start | bytes 196
  12.9 24.5 %all-to-all-start = ((bf16[16,8,4,576]{3,1,2,0:T(8,128)(2,1)}), bf16[16,8,4,576]{3,1,2,0:T(8,128)(2,1)S(1)}, u32[]{:S(2)}, u32[]{:S(2)}) async-start(bf16[16,8,4,576]{3,1,2,0:T(8,128)(2,1)} %convolution_convert_fusion.1), calls=%async_computation | async-start | bytes 1310720 | tf_op jit(solution)/shard_map/all_to_all | solution.py:244
  45.0 13.9 %copy-start.1 = (bf16[16,8,4,192]{3,2,1,0:T(4,128)(2,1)S(1)}, bf16[16,8,4,192]{3,2,1,0:T(4,128)(2,1)}, u32[]{:S(2)}) copy-start(bf16[16,8,4,192]{3,2,1,0:T(4,128)(2,1)} %param.8) | copy-start | bytes 589828
  45.0 13.9 %copy-start.11 = (bf16[192,192]{1,0:T(8,128)(2,1)S(1)}, bf16[192,192]{1,0:T(8,128)(2,1)}, u32[]{:S(2)}) copy-start(bf16[192,192]{1,0:T(8,128)(2,1)} %param.10) | copy-start | bytes 221188
  45.0 19.1 %copy-start.14 = (f32[3,3,3,192]{3,2,1,0:T(4,128)S(1)}, f32[3,3,3,192]{3,2,1,0:T(4,128)}, u32[]{:S(2)}) copy-start(f32[3,3,3,192]{3,2,1,0:T(4,128)} %param.11) | copy-start | bytes 62212
  59.3 7.0 %collective-permute-start = (bf16[16,1,4,192]{3,1,2,0:T(2,128)(2,1)S(1)}, bf16[16,1,4,192]{3,1,2,0:T(2,128)(2,1)S(1)}, u32[]{:S(2)}, u32[]{:S(2)}) collective-permute-start(bf16[16,1,4,192]{3,1,2,0:T(2,128)(2,1)S(1)} %get-tuple-element.97), channel_id=1, source_target_pairs={{0,4},{4,8},{8,12},{12,16},{16,20},{20,24},{24,28},{28,0},{1,5},{5... | collective-permute-start | bytes 73736 | tf_op jit(solution)/shard_map/ppermute | solution.py:22
  60.8 5.6 %collective-permute-start.1 = (bf16[16,1,4,192]{3,1,2,0:T(2,128)(2,1)S(1)}, bf16[16,1,4,192]{3,1,2,0:T(2,128)(2,1)S(1)}, u32[]{:S(2)}, u32[]{:S(2)}) collective-permute-start(bf16[16,1,4,192]{3,1,2,0:T(2,128)(2,1)S(1)} %get-tuple-element.98), channel_id=1, source_target_pairs={{4,0},{8,4},{12,8},{16,12},{20,16},{24,20},{28,24},{0,28},{5,1},{9... | collective-permute-start | bytes 73736 | tf_op jit(solution)/shard_map/ppermute | solution.py:24
  64.7 7.8 %copy-start.15 = (f32[1,1,1,192]{3,2,1,0:T(1,128)}, f32[1,1,1,192]{3,2,1,0:T(1,128)S(1)}, u32[]{:S(2)}) copy-start(f32[1,1,1,192]{3,2,1,0:T(1,128)S(1)} %get-tuple-element.99) | copy-start | bytes 2308
  64.7 7.8 %copy-start.17 = (f32[1,1,1,192]{3,2,1,0:T(1,128)}, f32[1,1,1,192]{3,2,1,0:T(1,128)S(1)}, u32[]{:S(2)}) copy-start(f32[1,1,1,192]{3,2,1,0:T(1,128)S(1)} %get-tuple-element.100) | copy-start | bytes 2308
  64.7 7.8 %copy-start.19 = (f32[1,1,1,192]{3,2,1,0:T(1,128)}, f32[1,1,1,192]{3,2,1,0:T(1,128)S(1)}, u32[]{:S(2)}) copy-start(f32[1,1,1,192]{3,2,1,0:T(1,128)S(1)} %get-tuple-element.101) | copy-start | bytes 2308
  64.7 7.8 %copy-start.21 = (f32[1,1,1,192]{3,2,1,0:T(1,128)}, f32[1,1,1,192]{3,2,1,0:T(1,128)S(1)}, u32[]{:S(2)}) copy-start(f32[1,1,1,192]{3,2,1,0:T(1,128)S(1)} %get-tuple-element.102) | copy-start | bytes 2308
  64.7 7.8 %copy-start.23 = (f32[1,1,1,192]{3,2,1,0:T(1,128)}, f32[1,1,1,192]{3,2,1,0:T(1,128)S(1)}, u32[]{:S(2)}) copy-start(f32[1,1,1,192]{3,2,1,0:T(1,128)S(1)} %get-tuple-element.103) | copy-start | bytes 2308
  64.7 7.8 %copy-start.25 = (f32[1,1,1,192]{3,2,1,0:T(1,128)}, f32[1,1,1,192]{3,2,1,0:T(1,128)S(1)}, u32[]{:S(2)}) copy-start(f32[1,1,1,192]{3,2,1,0:T(1,128)S(1)} %get-tuple-element.104) | copy-start | bytes 2308
  64.8 7.8 %copy-start.27 = (f32[1,1,1,192]{3,2,1,0:T(1,128)}, f32[1,1,1,192]{3,2,1,0:T(1,128)S(1)}, u32[]{:S(2)}) copy-start(f32[1,1,1,192]{3,2,1,0:T(1,128)S(1)} %get-tuple-element.105) | copy-start | bytes 2308
  66.5 4.4 %collective-permute-start.2 = (bf16[16,10,1,192]{3,1,2,0:T(8,128)(2,1)S(1)}, bf16[16,10,1,192]{3,1,2,0:T(8,128)(2,1)S(1)}, u32[]{:S(2)}, u32[]{:S(2)}) collective-permute-start(bf16[16,10,1,192]{3,1,2,0:T(8,128)(2,1)S(1)} %get-tuple-element.93), channel_id=1, source_target_pairs={{0,1},{1,2},{2,3},{3,0},{4,5},{5,6},{6,7},{7,4},{8,9},{9,10},{10,1... | collective-permute-start | bytes 184328 | tf_op jit(solution)/shard_map/ppermute | solution.py:22
  66.5 4.8 %collective-permute-start.3 = (bf16[16,10,1,192]{3,1,2,0:T(8,128)(2,1)S(1)}, bf16[16,10,1,192]{3,1,2,0:T(8,128)(2,1)S(1)}, u32[]{:S(2)}, u32[]{:S(2)}) collective-permute-start(bf16[16,10,1,192]{3,1,2,0:T(8,128)(2,1)S(1)} %get-tuple-element.94), channel_id=1, source_target_pairs={{1,0},{2,1},{3,2},{0,3},{5,4},{6,5},{7,6},{4,7},{9,8},{10,9},{11,1... | collective-permute-start | bytes 184328 | tf_op jit(solution)/shard_map/ppermute | solution.py:24
  78.3 7.2 %copy-start.3 = (f32[2,4,6,64,64]{3,4,2,1,0:T(8,128)S(1)}, f32[2,4,6,64,64]{3,4,2,1,0:T(8,128)}, u32[]{:S(2)}) copy-start(f32[2,4,6,64,64]{3,4,2,1,0:T(8,128)} %copy-done.2) | copy-start | bytes 2359300
  80.8 7.4 %collective-permute-start.4 = (bf16[16,1,4,192]{3,1,2,0:T(2,128)(2,1)}, bf16[16,1,4,192]{3,1,2,0:T(2,128)(2,1)S(1)}, u32[]{:S(2)}, u32[]{:S(2)}) collective-permute-start(bf16[16,1,4,192]{3,1,2,0:T(2,128)(2,1)} %get-tuple-element.95), channel_id=1, source_target_pairs={{0,4},{4,8},{8,12},{12,16},{16,20},{20,24},{24,28},{28,0},{1,5},{5... | collective-permute-start | bytes 73736 | tf_op jit(solution)/shard_map/ppermute | solution.py:22
  81.5 6.7 %collective-permute-start.5 = (bf16[16,1,4,192]{3,1,2,0:T(2,128)(2,1)}, bf16[16,1,4,192]{3,1,2,0:T(2,128)(2,1)S(1)}, u32[]{:S(2)}, u32[]{:S(2)}) collective-permute-start(bf16[16,1,4,192]{3,1,2,0:T(2,128)(2,1)} %get-tuple-element.96), channel_id=1, source_target_pairs={{4,0},{8,4},{12,8},{16,12},{20,16},{24,20},{28,24},{0,28},{5,1},{9... | collective-permute-start | bytes 73736 | tf_op jit(solution)/shard_map/ppermute | solution.py:24
  88.4 4.4 %collective-permute-start.6 = (bf16[16,10,1,192]{3,1,2,0:T(8,128)(2,1)S(1)}, bf16[16,10,1,192]{3,1,2,0:T(8,128)(2,1)S(1)}, u32[]{:S(2)}, u32[]{:S(2)}) collective-permute-start(bf16[16,10,1,192]{3,1,2,0:T(8,128)(2,1)S(1)} %get-tuple-element.89), channel_id=1, source_target_pairs={{0,1},{1,2},{2,3},{3,0},{4,5},{5,6},{6,7},{7,4},{8,9},{9,10},{10,1... | collective-permute-start | bytes 184328 | tf_op jit(solution)/shard_map/ppermute | solution.py:22
  89.0 4.8 %collective-permute-start.7 = (bf16[16,10,1,192]{3,1,2,0:T(8,128)(2,1)S(1)}, bf16[16,10,1,192]{3,1,2,0:T(8,128)(2,1)S(1)}, u32[]{:S(2)}, u32[]{:S(2)}) collective-permute-start(bf16[16,10,1,192]{3,1,2,0:T(8,128)(2,1)S(1)} %get-tuple-element.90), channel_id=1, source_target_pairs={{1,0},{2,1},{3,2},{0,3},{5,4},{6,5},{7,6},{4,7},{9,8},{10,9},{11,1... | collective-permute-start | bytes 184328 | tf_op jit(solution)/shard_map/ppermute | solution.py:24
  98.4 55.9 %all-to-all-start.2 = ((bf16[16,8,4,192]{3,1,2,0:T(8,128)(2,1)}), bf16[16,8,4,192]{3,1,2,0:T(8,128)(2,1)}, u32[]{:S(2)}, u32[]{:S(2)}) async-start(bf16[16,8,4,192]{3,1,2,0:T(8,128)(2,1)} %convolution_convert_fusion.4), calls=%async_computation.2 | async-start | bytes 524288 | tf_op jit(solution)/shard_map/all_to_all | solution.py:261
  104.1 3.2 copy-start.69
  104.1 3.2 copy-start.70
  104.1 3.2 copy-start.71
  104.2 47.5 %copy-start.6 = (f32[16,8,4,768]{3,1,2,0:T(8,128)S(1)}, f32[16,8,4,768]{3,1,2,0:T(8,128)}, u32[]{:S(2)}) copy-start(f32[16,8,4,768]{3,1,2,0:T(8,128)} %copy-done.5) | copy-start | bytes 4718596
  173.9 7.2 %copy-start.88 = (bf16[16,8,4,768]{3,1,2,0:T(8,128)(2,1)S(1)}, bf16[16,8,4,768]{3,1,2,0:T(8,128)(2,1)}, u32[]{:S(2)}) copy-start(bf16[16,8,4,768]{3,1,2,0:T(8,128)(2,1)} %copy-done.87) | copy-start | bytes 2359300
  175.2 20.8 %all-to-all-start.3 = ((bf16[2,64,4,576]{3,2,0,1:T(4,128)(2,1)}), bf16[2,64,4,576]{3,2,0,1:T(4,128)(2,1)S(1)}, u32[]{:S(2)}, u32[]{:S(2)}) async-start(bf16[2,64,4,576]{3,2,0,1:T(4,128)(2,1)} %copy.120), calls=%async_computation.3 | async-start | bytes 1310720 | tf_op jit(solution)/shard_map/all_to_all | solution.py:263
  180.4 151.3 %all-reduce.5.cloned.1.call-start = ((), (), s32[]{:S(2)}) async-start(), calls=%async_computation.4 | async-start | bytes 3735552 | tf_op jit(solution)/shard_map/psum | solution.py:270
  331.8 3.6 %copy-start.10 = (f32[192,768]{1,0:T(8,128)S(1)}, f32[192,768]{1,0:T(8,128)}, u32[]{:S(2)}) copy-start(f32[192,768]{1,0:T(8,128)} %get-tuple-element.78) | copy-start | bytes 1769476
  331.8 4.4 %copy-start.9 = (f32[768,192]{0,1:T(8,128)S(1)}, f32[768,192]{0,1:T(8,128)}, u32[]{:S(2)}) copy-start(f32[768,192]{0,1:T(8,128)} %get-tuple-element.79) | copy-start | bytes 1769476
  (69 other events, 187.1 us)
Sparse Core Ops, SparseCore 0:
  198.9 132.8 all-reduce.4
where the time goes:
time: 345 us; the launch traced here: 344 us
  waiting for transfers between devices  165 us (48%)
  blocking collectives  54.1 us (16%)
  starting transfers between devices  31.3 us (9%)
  matrix products  29.4 us (9%)
  other arithmetic  24.1 us (7%)
  local copies, waits for them, and re-layouts  24 us (7%)
  between operations  15.6 us (5%)
    psum x1, waiting for transfers between devices, local(): lax.psum((part_qkv, part_out, part_kernel, part_up, part_down), ('gy', 'g...  131 us
    psum x1, blocking collectives, local(): lax.psum((part_qkv, part_out, part_kernel, part_up, part_down), ('gy', 'g...  41.6 us
    all_to_all x1, waiting for transfers between devices, local(): lax.all_to_all(qkv_rows, 'gy', split_axis=0, concat_axis=1, tiled=True)  17 us
    dot_general x6, matrix products, head_product(): jnp.einsum(einsum_form, left_side, right_side, preferred_element_type=jnp...  15.5 us
    all_to_all x1, blocking collectives, attention_exchange_back(): lax.all_to_all(attend(qkv_lines, mask_full, HEADS), 'gy', split_axis=1, c...  12.5 us
    all_to_all x1, waiting for transfers between devices, local(): lax.all_to_all(grad_qkv_lines, 'gy', split_axis=1, concat_axis=0, tiled=T...  12.4 us
    ppermute x4, starting transfers between devices, with_halo(): lax.ppermute(head, axis, [((i + 1) % count, i) for i in range(count)])  10.2 us
    all_to_all x1, starting transfers between devices, local(): lax.all_to_all(qkv_rows, 'gy', split_axis=0, concat_axis=1, tiled=True)  7.25 us
  transfers between devices with their start and end apart: 12, of which 9 were waited for; matrix products, arithmetic and copies ran while one was open for 6% of the time, Pallas kernels for 0%

commit v1 on v0

--- a/solution.py
+++ b/solution.py
@@ -267,7 +267,9 @@
         grad_value.astype(jnp.float32)
         + norm_rows_back(grad_normed.astype(jnp.float32), normal_first, inverse_first)
     ).astype(jnp.bfloat16)
-    summed_parts = lax.psum((part_qkv, part_out, part_kernel, part_up, part_down), ("gy", "gz"))
+    summed_parts = lax.psum(
+        lax.psum((part_qkv, part_out, part_kernel, part_up, part_down), "gz"), "gy"
+    )
     token_count = (
         tokens.shape[0]
         * tokens.shape[1]

time: 345 us -> 323 us (0.936)
  waiting for transfers between devices: 165 us -> 136 us
  blocking collectives: 54.1 us -> 62.1 us
  local copies, waits for them, and re-layouts: 24 us -> 19.7 us
  matrix products: 29.4 us -> 33.6 us
    psum x1 -> x2, waiting for transfers between devices: 131 us -> 92.3 us  [the longest x1 46.6 us: local(): lax.psum((part_qkv, part_out, part_kernel, part_up, part_down), 'gz')]
    psum x1 -> x2, blocking collectives: 41.6 us -> 49.6 us  [the longest x1 38.6 us: local(): lax.psum(lax.psum((part_qkv, part_out, part_kernel, part_up, part_down),...]
    ppermute x4, waiting for transfers between devices: 3.31 us -> 9.78 us  [with_halo(): lax.ppermute(tail, axis, [(i, (i + 1) % count) for i in range(count)])]
    all_to_all x1, waiting for transfers between devices: 0.01 us -> 4.95 us  [local(): lax.all_to_all(grad_attended, 'gy', split_axis=0, concat_axis=1, tiled=True)]
  transfers between devices with their start and end apart: 12 -> 13, of which waited for: 9 -> 11; matrix products, arithmetic and copies ran while one was open for 6% -> 6% of each run, Pallas kernels for 0% -> 0%
where the time goes in v1:
time: 323 us; the launch traced here: 322 us
  waiting for transfers between devices  136 us (42%)
  blocking collectives  62.1 us (19%)
  matrix products  33.6 us (10%)
  starting transfers between devices  30.3 us (9%)
  other arithmetic  25.4 us (8%)
  local copies, waits for them, and re-layouts  19.7 us (6%)
  between operations  14.9 us (5%)
    psum x1, waiting for transfers between devices, local(): lax.psum((part_qkv, part_out, part_kernel, part_up, part_down), 'gz')  46.6 us
    psum x1, waiting for transfers between devices, local(): lax.psum(lax.psum((part_qkv, part_out, part_kernel, part_up, part_down),...  45.7 us
    psum x1, blocking collectives, local(): lax.psum(lax.psum((part_qkv, part_out, part_kernel, part_up, part_down),...  38.6 us
    dot_general x6, matrix products, head_product(): jnp.einsum(einsum_form, left_side, right_side, preferred_element_type=jnp...  17.4 us
    all_to_all x1, waiting for transfers between devices, local(): lax.all_to_all(qkv_rows, 'gy', split_axis=0, concat_axis=1, tiled=True)  17 us
    all_to_all x1, blocking collectives, attention_exchange_back(): lax.all_to_all(attend(qkv_lines, mask_full, HEADS), 'gy', split_axis=1, c...  12.5 us
    psum x1, blocking collectives, local(): lax.psum((part_qkv, part_out, part_kernel, part_up, part_down), 'gz')  10.9 us
    ppermute x4, starting transfers between devices, with_halo(): lax.ppermute(head, axis, [((i + 1) % count, i) for i in range(count)])  10.8 us
  transfers between devices with their start and end apart: 13, of which 11 were waited for; matrix products, arithmetic and copies ran while one was open for 6% of the time, Pallas kernels for 0%

profile of v1, /device:TPU:0, one launch (start us, length us, event | category | flops | bytes accessed | tf_op | source)
XLA Modules:
  0.0 321.7 jit_solution(15763534790120230218)
XLA Ops:
  10.8 2.1 convolution_convert_fusion.1
  13.0 7.3 %all-to-all-start = ((bf16[16,8,4,576]{3,1,2,0:T(8,128)(2,1)}), bf16[16,8,4,576]{3,1,2,0:T(8,128)(2,1)S(1)}, u32[]{:S(2)}, u32[]{:S(2)}) async-start(bf16[16,8,4,576]{3,1,2,0:T(8,128)(2,1)} %convolution_convert_fusion.1), calls=%async_computation | async-start | bytes 1310720 | tf_op jit(solution)/shard_map/all_to_all | solution.py:244
  20.5 17.0 %all-to-all-done = bf16[16,8,4,576]{3,1,2,0:T(8,128)(2,1)S(1)} async-done(((bf16[16,8,4,576]{3,1,2,0:T(8,128)(2,1)}), bf16[16,8,4,576]{3,1,2,0:T(8,128)(2,1)S(1)}, u32[]{:S(2)}, u32[]{:S(2)}) %all-to-all-start) | async-done | bytes 589856 | tf_op jit(solution)/shard_map/all_to_all | solution.py:244
  40.6 2.2 convolution_convert_fusion.3
  43.2 12.5 %all_to_all.63 = bf16[2,64,4,192]{3,2,0,1:T(4,128)(2,1)S(1)} all-to-all(bf16[2,64,4,192]{3,2,0,1:T(4,128)(2,1)S(1)} %copy.104), channel_id=1, replica_groups=mesh['gy'=8,'gz'=4] {'gy'}, dimensions={1} | all-to-all | bytes 393216 | tf_op jit(solution)/shard_map/all_to_all | solution.py:216
  57.6 3.3 %collective-permute-start.1 = (bf16[16,1,4,192]{3,1,2,0:T(2,128)(2,1)S(1)}, bf16[16,1,4,192]{3,1,2,0:T(2,128)(2,1)S(1)}, u32[]{:S(2)}, u32[]{:S(2)}) collective-permute-start(bf16[16,1,4,192]{3,1,2,0:T(2,128)(2,1)S(1)} %get-tuple-element.102), channel_id=1, source_target_pairs={{4,0},{8,4},{12,8},{16,12},{20,16},{24,20},{28,24},{0,28},{5,1},{9... | collective-permute-start | bytes 73736 | tf_op jit(solution)/shard_map/ppermute | solution.py:24
  60.9 2.2 collective-permute-done
  63.4 1.7 collective-permute-start.3
  65.1 2.6 collective-permute-done.2
  69.4 2.4 convert_reduce_fusion
  75.0 1.7 fusion.121
  77.6 4.1 %collective-permute-start.5 = (bf16[16,1,4,192]{3,1,2,0:T(2,128)(2,1)S(1)}, bf16[16,1,4,192]{3,1,2,0:T(2,128)(2,1)S(1)}, u32[]{:S(2)}, u32[]{:S(2)}) collective-permute-start(bf16[16,1,4,192]{3,1,2,0:T(2,128)(2,1)S(1)} %get-tuple-element.100), channel_id=1, source_target_pairs={{4,0},{8,4},{12,8},{16,12},{20,16},{24,20},{28,24},{0,28},{5,1},{9... | collective-permute-start | bytes 73736 | tf_op jit(solution)/shard_map/ppermute | solution.py:24
  81.7 2.4 collective-permute-done.4
  86.2 2.5 collective-permute-done.6
  90.9 2.2 fusion.132
  94.7 5.8 %all-to-all-start.2 = ((bf16[16,8,4,192]{3,1,2,0:T(8,128)(2,1)}), bf16[16,8,4,192]{3,1,2,0:T(8,128)(2,1)S(1)}, u32[]{:S(2)}, u32[]{:S(2)}) async-start(bf16[16,8,4,192]{3,1,2,0:T(8,128)(2,1)} %convolution_convert_fusion.4), calls=%async_computation.2 | async-start | bytes 524288 | tf_op jit(solution)/shard_map/all_to_all | solution.py:261
  101.5 3.2 fusion.27
  105.8 5.0 %all-to-all-done.2 = bf16[16,8,4,192]{3,1,2,0:T(8,128)(2,1)S(1)} async-done(((bf16[16,8,4,192]{3,1,2,0:T(8,128)(2,1)}), bf16[16,8,4,192]{3,1,2,0:T(8,128)(2,1)S(1)}, u32[]{:S(2)}, u32[]{:S(2)}) %all-to-all-start.2) | async-done | bytes 196640 | tf_op jit(solution)/shard_map/all_to_all | solution.py:261
  114.3 3.4 %convolution_convert_fusion.2 = bf16[2,4,6,32,64]{4,3,2,1,0:T(8,128)(2,1)} fusion(bf16[2,64,4,6,32]{1,4,3,2,0:T(8,128)(2,1)} %copy.110, f32[2,4,6,64,64]{3,4,2,1,0:T(8,128)} %exponential_multiply_fusion), kind=kOutput, calls=%fused_computation.52 | convolution fusion | flops 13077567 | bytes 1179648 | tf_op jit(solution)/shard_map/abhij,aibhd->ajbhd/dot_general | solution.py:104
  119.2 4.3 %fusion.16 = f32[2,4,6,32,64]{4,3,2,1,0:T(8,128)} fusion(bf16[2,64,4,6,32]{1,4,3,2,0:T(8,128)(2,1)S(1)} %bitcast.171, f32[2,4,6,64,64]{3,4,2,1,0:T(8,128)} %fusion.27, f32[2,4,6,64,64]{3,4,2,1,0:T(8,128)} %fusion.163), kind=kOutput, calls=%fused_computation.48 | convolution fusion | flops 13569087 | bytes 2162688 | tf_op jit(solution)/shard_map/abhij,ajbhd->aibhd/dot_general | solution.py:104
  123.5 4.3 %fusion.13 = f32[2,4,6,32,64]{4,3,2,1,0:T(8,128)} fusion(bf16[2,64,4,6,32]{1,4,3,2,0:T(8,128)(2,1)S(1)} %bitcast.173, f32[2,4,6,64,64]{3,4,2,1,0:T(8,128)} %fusion.27, f32[2,4,6,64,64]{3,4,2,1,0:T(8,128)} %fusion.163), kind=kOutput, calls=%fused_computation.47 | convolution fusion | flops 13569087 | bytes 2162688 | tf_op jit(solution)/shard_map/abhij,aibhd->ajbhd/dot_general | solution.py:104
  134.3 3.6 %all-to-all-start.3 = ((bf16[2,64,4,576]{3,2,0,1:T(4,128)(2,1)}), bf16[2,64,4,576]{3,2,0,1:T(4,128)(2,1)S(1)}, u32[]{:S(2)}, u32[]{:S(2)}) async-start(bf16[2,64,4,576]{3,2,0,1:T(4,128)(2,1)} %copy.120), calls=%async_computation.3 | async-start | bytes 1310720 | tf_op jit(solution)/shard_map/all_to_all | solution.py:263
  138.0 3.0 convolution_bitcast_fusion.1
  143.4 1.9 fusion.165
  145.2 10.3 %all-to-all-done.3 = bf16[2,64,4,576]{3,2,0,1:T(4,128)(2,1)S(1)} async-done(((bf16[2,64,4,576]{3,2,0,1:T(4,128)(2,1)}), bf16[2,64,4,576]{3,2,0,1:T(4,128)(2,1)S(1)}, u32[]{:S(2)}, u32[]{:S(2)}) %all-to-all-start.3) | async-done | bytes 589856 | tf_op jit(solution)/shard_map/all_to_all | solution.py:263
  158.5 2.1 fusion.164
  160.8 46.6 %all-reduce.9.cloned.1.call-done = (f32[192,576]{1,0:T(8,128)}, f32[192,192]{1,0:T(8,128)}, f32[192,768]{1,0:T(8,128)}, f32[768,192]{0,1:T(8,128)}) async-done(((f32[192,576]{1,0:T(8,128)}, f32[192,192]{1,0:T(8,128)}, f32[192,768]{1,0:T(8,128)}, f32[768,192]{0,1:T(8,128)}), (f32[192,576]{1,0:T(8,128)}, f32[192,192]{1,0:T(8,128)}, f32[192,768]{1,0:T(8,128)}, ...) | async-done | bytes 1769488 | tf_op jit(solution)/shard_map/psum | solution.py:271
  207.5 2.0 fusion.18
  211.9 10.9 %psum.74 = f32[3,3,3,192]{3,2,1,0:T(4,128)S(1)} all-reduce(f32[3,3,3,192]{3,2,1,0:T(4,128)S(1)} %reshape.191), channel_id=1, replica_groups=mesh['gy'=8,'gz'=4] {'gz'}, use_global_device_ids=true, to_apply=%region_45.46 | all-reduce | flops 5184 | bytes 41472 | tf_op jit(solution)/shard_map/psum | solution.py:271
  222.8 38.6 %psum.75 = f32[3,3,3,192]{3,2,1,0:T(4,128)S(1)} all-reduce(f32[3,3,3,192]{3,2,1,0:T(4,128)S(1)} %psum.74), channel_id=1, replica_groups=mesh['gy'=8,'gz'=4] {'gy'}, use_global_device_ids=true, to_apply=%region_46.47 | all-reduce | flops 5184 | bytes 41472 | tf_op jit(solution)/shard_map/psum | solution.py:270
  263.9 45.7 %all-reduce.7.cloned.1.call-done = (f32[192,576]{1,0:T(8,128)}, f32[192,192]{1,0:T(8,128)}, f32[192,768]{1,0:T(8,128)}, f32[768,192]{0,1:T(8,128)}) async-done(((f32[192,576]{1,0:T(8,128)}, f32[192,192]{1,0:T(8,128)}, f32[192,768]{1,0:T(8,128)}, f32[768,192]{0,1:T(8,128)}), (f32[192,576]{1,0:T(8,128)}, f32[192,192]{1,0:T(8,128)}, f32[192,768]{1,0:T(8,128)}, ...) | async-done | bytes 1769488 | tf_op jit(solution)/shard_map/psum | solution.py:270
  309.6 1.9 broadcast_multiply_fusion.2
  (183 shorter events, 47.9 us)
Async XLA Ops:
  7.2 65.0 %copy-start = (bf16[192,768]{1,0:T(8,128)(2,1)S(1)}, bf16[192,768]{1,0:T(8,128)(2,1)}, u32[]{:S(2)}) copy-start(bf16[192,768]{1,0:T(8,128)(2,1)} %param.12) | copy-start | bytes 884740
  8.4 4.6 %copy-start.20 = (f32[16,8,4]{1,2,0:T(4,128)}, f32[16,8,4]{1,2,0:T(4,128)S(1)}, u32[]{:S(2)}) copy-start(f32[16,8,4]{1,2,0:T(4,128)S(1)} %broadcast_multiply_fusion.10) | copy-start | bytes 6148
  9.6 10.6 %copy-start.41 = (s32[4,4]{1,0:T(4,128)S(1)}, s32[4,4]{1,0:T(4,128)}, u32[]{:S(2)}) copy-start(s32[4,4]{1,0:T(4,128)} %param.14) | copy-start | bytes 196
  9.6 3.3 %copy-start.26 = (f32[16,8,4]{1,2,0:T(4,128)}, f32[16,8,4]{1,2,0:T(4,128)S(1)}, u32[]{:S(2)}) copy-start(f32[16,8,4]{1,2,0:T(4,128)S(1)} %add_rsqrt_fusion.1) | copy-start | bytes 6148
  13.0 24.6 %all-to-all-start = ((bf16[16,8,4,576]{3,1,2,0:T(8,128)(2,1)}), bf16[16,8,4,576]{3,1,2,0:T(8,128)(2,1)S(1)}, u32[]{:S(2)}, u32[]{:S(2)}) async-start(bf16[16,8,4,576]{3,1,2,0:T(8,128)(2,1)} %convolution_convert_fusion.1), calls=%async_computation | async-start | bytes 1310720 | tf_op jit(solution)/shard_map/all_to_all | solution.py:244
  39.0 3.9 %copy-start.10 = (bf16[2,64,4,192]{1,3,2,0:T(8,128)(2,1)}, bf16[2,64,4,192]{1,3,2,0:T(8,128)(2,1)S(1)}, u32[]{:S(2)}) copy-start(bf16[2,64,4,192]{1,3,2,0:T(8,128)(2,1)S(1)} %copy.101) | copy-start | bytes 589828
  42.9 12.9 %copy-start.1 = (bf16[16,8,4,192]{3,2,1,0:T(4,128)(2,1)S(1)}, bf16[16,8,4,192]{3,2,1,0:T(4,128)(2,1)}, u32[]{:S(2)}) copy-start(bf16[16,8,4,192]{3,2,1,0:T(4,128)(2,1)} %param.8) | copy-start | bytes 589828
  42.9 12.9 %copy-start.22 = (bf16[192,192]{1,0:T(8,128)(2,1)S(1)}, bf16[192,192]{1,0:T(8,128)(2,1)}, u32[]{:S(2)}) copy-start(bf16[192,192]{1,0:T(8,128)(2,1)} %param.10) | copy-start | bytes 221188
  42.9 18.0 %copy-start.31 = (f32[3,3,3,192]{3,2,1,0:T(4,128)S(1)}, f32[3,3,3,192]{3,2,1,0:T(4,128)}, u32[]{:S(2)}) copy-start(f32[3,3,3,192]{3,2,1,0:T(4,128)} %param.11) | copy-start | bytes 62212
  56.1 7.0 %collective-permute-start = (bf16[16,1,4,192]{3,1,2,0:T(2,128)(2,1)S(1)}, bf16[16,1,4,192]{3,1,2,0:T(2,128)(2,1)S(1)}, u32[]{:S(2)}, u32[]{:S(2)}) collective-permute-start(bf16[16,1,4,192]{3,1,2,0:T(2,128)(2,1)S(1)} %get-tuple-element.101), channel_id=1, source_target_pairs={{0,4},{4,8},{8,12},{12,16},{16,20},{20,24},{24,28},{28,0},{1,5},{5... | collective-permute-start | bytes 73736 | tf_op jit(solution)/shard_map/ppermute | solution.py:22
  57.6 5.6 %collective-permute-start.1 = (bf16[16,1,4,192]{3,1,2,0:T(2,128)(2,1)S(1)}, bf16[16,1,4,192]{3,1,2,0:T(2,128)(2,1)S(1)}, u32[]{:S(2)}, u32[]{:S(2)}) collective-permute-start(bf16[16,1,4,192]{3,1,2,0:T(2,128)(2,1)S(1)} %get-tuple-element.102), channel_id=1, source_target_pairs={{4,0},{8,4},{12,8},{16,12},{20,16},{24,20},{28,24},{0,28},{5,1},{9... | collective-permute-start | bytes 73736 | tf_op jit(solution)/shard_map/ppermute | solution.py:24
  63.3 4.4 %collective-permute-start.2 = (bf16[16,10,1,192]{3,1,2,0:T(8,128)(2,1)S(1)}, bf16[16,10,1,192]{3,1,2,0:T(8,128)(2,1)S(1)}, u32[]{:S(2)}, u32[]{:S(2)}) collective-permute-start(bf16[16,10,1,192]{3,1,2,0:T(8,128)(2,1)S(1)} %get-tuple-element.97), channel_id=1, source_target_pairs={{0,1},{1,2},{2,3},{3,0},{4,5},{5,6},{6,7},{7,4},{8,9},{9,10},{10,1... | collective-permute-start | bytes 184328 | tf_op jit(solution)/shard_map/ppermute | solution.py:22
  63.4 4.8 %collective-permute-start.3 = (bf16[16,10,1,192]{3,1,2,0:T(8,128)(2,1)S(1)}, bf16[16,10,1,192]{3,1,2,0:T(8,128)(2,1)S(1)}, u32[]{:S(2)}, u32[]{:S(2)}) collective-permute-start(bf16[16,10,1,192]{3,1,2,0:T(8,128)(2,1)S(1)} %get-tuple-element.98), channel_id=1, source_target_pairs={{1,0},{2,1},{3,2},{0,3},{5,4},{6,5},{7,6},{4,7},{9,8},{10,9},{11,1... | collective-permute-start | bytes 184328 | tf_op jit(solution)/shard_map/ppermute | solution.py:24
  76.8 7.3 %collective-permute-start.4 = (bf16[16,1,4,192]{3,1,2,0:T(2,128)(2,1)S(1)}, bf16[16,1,4,192]{3,1,2,0:T(2,128)(2,1)S(1)}, u32[]{:S(2)}, u32[]{:S(2)}) collective-permute-start(bf16[16,1,4,192]{3,1,2,0:T(2,128)(2,1)S(1)} %get-tuple-element.99), channel_id=1, source_target_pairs={{0,4},{4,8},{8,12},{12,16},{16,20},{20,24},{24,28},{28,0},{1,5},{5... | collective-permute-start | bytes 73736 | tf_op jit(solution)/shard_map/ppermute | solution.py:22
  77.6 6.5 %collective-permute-start.5 = (bf16[16,1,4,192]{3,1,2,0:T(2,128)(2,1)S(1)}, bf16[16,1,4,192]{3,1,2,0:T(2,128)(2,1)S(1)}, u32[]{:S(2)}, u32[]{:S(2)}) collective-permute-start(bf16[16,1,4,192]{3,1,2,0:T(2,128)(2,1)S(1)} %get-tuple-element.100), channel_id=1, source_target_pairs={{4,0},{8,4},{12,8},{16,12},{20,16},{24,20},{28,24},{0,28},{5,1},{9... | collective-permute-start | bytes 73736 | tf_op jit(solution)/shard_map/ppermute | solution.py:24
  84.3 4.4 %collective-permute-start.6 = (bf16[16,10,1,192]{3,1,2,0:T(8,128)(2,1)S(1)}, bf16[16,10,1,192]{3,1,2,0:T(8,128)(2,1)S(1)}, u32[]{:S(2)}, u32[]{:S(2)}) collective-permute-start(bf16[16,10,1,192]{3,1,2,0:T(8,128)(2,1)S(1)} %get-tuple-element.93), channel_id=1, source_target_pairs={{0,1},{1,2},{2,3},{3,0},{4,5},{5,6},{6,7},{7,4},{8,9},{9,10},{10,1... | collective-permute-start | bytes 184328 | tf_op jit(solution)/shard_map/ppermute | solution.py:22
  84.6 5.1 %collective-permute-start.7 = (bf16[16,10,1,192]{3,1,2,0:T(8,128)(2,1)S(1)}, bf16[16,10,1,192]{3,1,2,0:T(8,128)(2,1)S(1)}, u32[]{:S(2)}, u32[]{:S(2)}) collective-permute-start(bf16[16,10,1,192]{3,1,2,0:T(8,128)(2,1)S(1)} %get-tuple-element.94), channel_id=1, source_target_pairs={{1,0},{2,1},{3,2},{0,3},{5,4},{6,5},{7,6},{4,7},{9,8},{10,9},{11,1... | collective-permute-start | bytes 184328 | tf_op jit(solution)/shard_map/ppermute | solution.py:24
  94.7 16.0 %all-to-all-start.2 = ((bf16[16,8,4,192]{3,1,2,0:T(8,128)(2,1)}), bf16[16,8,4,192]{3,1,2,0:T(8,128)(2,1)S(1)}, u32[]{:S(2)}, u32[]{:S(2)}) async-start(bf16[16,8,4,192]{3,1,2,0:T(8,128)(2,1)} %convolution_convert_fusion.4), calls=%async_computation.2 | async-start | bytes 524288 | tf_op jit(solution)/shard_map/all_to_all | solution.py:261
  114.3 3.4 %copy-start.7 = (bf16[2,64,4,192]{1,3,2,0:T(8,128)(2,1)S(1)}, bf16[2,64,4,192]{1,3,2,0:T(8,128)(2,1)}, u32[]{:S(2)}) copy-start(bf16[2,64,4,192]{1,3,2,0:T(8,128)(2,1)} %copy-done.6) | copy-start | bytes 589828
  114.3 3.4 %copy-start.12 = (bf16[2,64,4,6,32]{1,4,3,2,0:T(8,128)(2,1)S(1)}, bf16[2,64,4,6,32]{1,4,3,2,0:T(8,128)(2,1)}, u32[]{:S(2)}) copy-start(bf16[2,64,4,6,32]{1,4,3,2,0:T(8,128)(2,1)} %copy.110) | copy-start | bytes 589828
  119.2 4.3 %copy-start.11 = (bf16[2,64,4,192]{1,3,2,0:T(8,128)(2,1)S(1)}, bf16[2,64,4,192]{1,3,2,0:T(8,128)(2,1)}, u32[]{:S(2)}) copy-start(bf16[2,64,4,192]{1,3,2,0:T(8,128)(2,1)} %copy-done.10) | copy-start | bytes 589828
  123.5 4.3 %copy-start.23 = (bf16[2,4,6,32,64]{4,3,2,1,0:T(8,128)(2,1)S(1)}, bf16[2,4,6,32,64]{4,3,2,1,0:T(8,128)(2,1)}, u32[]{:S(2)}) copy-start(bf16[2,4,6,32,64]{4,3,2,1,0:T(8,128)(2,1)} %convolution_convert_fusion.2) | copy-start | bytes 589828
  132.9 5.1 %copy-start.29 = (bf16[16,8,4,192]{3,2,1,0:T(4,128)(2,1)S(1)}, bf16[16,8,4,192]{3,2,1,0:T(4,128)(2,1)}, u32[]{:S(2)}) copy-start(bf16[16,8,4,192]{3,2,1,0:T(4,128)(2,1)} %param.15) | copy-start | bytes 589828
  134.3 21.3 %all-to-all-start.3 = ((bf16[2,64,4,576]{3,2,0,1:T(4,128)(2,1)}), bf16[2,64,4,576]{3,2,0,1:T(4,128)(2,1)S(1)}, u32[]{:S(2)}, u32[]{:S(2)}) async-start(bf16[2,64,4,576]{3,2,0,1:T(4,128)(2,1)} %copy.120), calls=%async_computation.3 | async-start | bytes 1310720 | tf_op jit(solution)/shard_map/all_to_all | solution.py:263
  137.9 69.5 %all-reduce.9.cloned.1.call-start = ((), (), s32[]{:S(2)}) async-start(), calls=%async_computation.5 | async-start | bytes 3735552 | tf_op jit(solution)/shard_map/psum | solution.py:271
  160.5 47.0 %copy-start.43 = (bf16[768,192]{0,1:T(8,128)(2,1)S(1)}, bf16[768,192]{0,1:T(8,128)(2,1)}, u32[]{:S(2)}) copy-start(bf16[768,192]{0,1:T(8,128)(2,1)} %param.13) | copy-start | bytes 884740
  160.6 149.0 %all-reduce.7.cloned.1.call-start = ((), (), s32[]{:S(2)}) async-start(), calls=%async_computation.4 | async-start | bytes 3735552 | tf_op jit(solution)/shard_map/psum | solution.py:270
  211.7 50.5 %copy-start.21 = (f32[16,8,4]{1,2,0:T(4,128)S(1)}, f32[16,8,4]{1,2,0:T(4,128)}, u32[]{:S(2)}) copy-start(f32[16,8,4]{1,2,0:T(4,128)} %copy-done.20) | copy-start | bytes 6148
  211.7 50.5 %copy-start.27 = (f32[16,8,4]{1,2,0:T(4,128)S(1)}, f32[16,8,4]{1,2,0:T(4,128)}, u32[]{:S(2)}) copy-start(f32[16,8,4]{1,2,0:T(4,128)} %copy-done.26) | copy-start | bytes 6148
  211.7 50.5 %copy-start.30 = (bf16[192,576]{1,0:T(8,128)(2,1)S(1)}, bf16[192,576]{1,0:T(8,128)(2,1)}, u32[]{:S(2)}) copy-start(bf16[192,576]{1,0:T(8,128)(2,1)} %param.9) | copy-start | bytes 663556
  309.6 3.6 %copy-start.17 = (f32[192,768]{1,0:T(8,128)S(1)}, f32[192,768]{1,0:T(8,128)}, u32[]{:S(2)}) copy-start(f32[192,768]{1,0:T(8,128)} %get-tuple-element.78) | copy-start | bytes 1769476
  309.6 4.4 %copy-start.16 = (f32[768,192]{0,1:T(8,128)S(1)}, f32[768,192]{0,1:T(8,128)}, u32[]{:S(2)}) copy-start(f32[768,192]{0,1:T(8,128)} %get-tuple-element.79) | copy-start | bytes 1769476
  (27 other events, 49.1 us)
Sparse Core Ops, SparseCore 0:
  160.7 46.7 all-reduce.8
  211.4 98.1 all-reduce.6
